TPU v7x, 256 devices: a whole 4x4x8 slice. The times are simulated.
256 devices in a mesh: dp: 64 (over z, y, core), mp: 4 (over x).
Axes of the slice: x: 4, y: 4, z: 8, core: 2. Of those that a mesh axis runs over, the one named last changes fastest.
Arguments:
- tokens: bfloat16 [49152, 768], P(('dp', 'mp')), may hold values from -6 to 6
- obs_mask: int32 [768, 64], P(('dp', 'mp')), may hold values 0 or 1
- norm_gains: float32 [5, 768], replicated, may hold values from 0.1 to 1.9
- attn_in: bfloat16 [2, 3, 768, 768], P(None, None, 'dp', 'mp'), may hold values from -0.21875 to 0.21875
- attn_out: bfloat16 [2, 768, 768], P(None, 'mp', 'dp'), may hold values from -0.21875 to 0.21875
- mlp_in: bfloat16 [2, 768, 3072], P(None, 'dp', 'mp'), may hold values from -0.21875 to 0.21875
- mlp_out: bfloat16 [2, 3072, 768], P(None, 'mp', 'dp'), may hold values from -0.109375 to 0.109375
- embodiment: int32 [768, 1], P('dp'), may hold values from 0 to 24; in each aligned block of 12 rows (0 to 11, 12 to 23, ...) no two rows name the same one
- levels: int32 [768, 2], P('dp'), may hold values from 0 to 19
- actions: bfloat16 [768, 2, 56], P('dp'), may hold values from -1 to 1
- noise: bfloat16 [768, 2, 56], P('dp'), may hold values from -5 to 5
- action_dims: int32 [25], replicated, may hold values from 7 to 14
- head_read: bfloat16 [64, 768, 256], P('dp'), may hold values from -0.21875 to 0.21875
- head_act: bfloat16 [64, 56, 256], P('dp'), may hold values from -0.75 to 0.75
- time_table: bfloat16 [64, 20, 256], P('dp'), may hold values from -5 to 5
- block_in: bfloat16 [64, 256, 256], P('dp'), may hold values from -0.375 to 0.375
- block_out: bfloat16 [64, 256, 256], P('dp'), may hold values from -0.375 to 0.375
- head_out: bfloat16 [64, 256, 56], P('dp'), may hold values from -0.375 to 0.375
Outputs:
- readout_grad: bfloat16 [768, 2, 768], P(('dp', 'mp'))
- grad_read: float32 [64, 768, 256], P('dp', 'mp')
- grad_act: float32 [64, 56, 256], P('dp')
- grad_time: float32 [64, 20, 256], P('dp')
- grad_block_in: float32 [64, 256, 256], P('dp')
- grad_block_out: float32 [64, 256, 256], P('dp')
- grad_head_out: float32 [64, 256, 56], P('dp')
Inputs may be any that keep to these rules, and one draw needn't show every extreme that they name: Within each aligned block of 12 samples (those of one dp index) no embodiment appears twice; every embodiment appears in some block.
All inputs are finite; a program needn't handle non-finite values. No bound on the sum of `obs_mask` on one device may be relied on, other than what follows from the above.
Results may differ from a plain program's by a relative error of at most 0.024.
Values may be sent and summed in bfloat16 or wider, within the bound.
No kernel may reach another device: no remote copies, remote signals or barrier semaphores. Data moves between devices by JAX's collectives and lax.ppermute only.
A program may use at most 64 MiB of HBM per device.

v0:
```python
import math
import jax
import jax.numpy as jnp
from jax import lax
from jax.sharding import Mesh, PartitionSpec as P

D = 768
HDIM = 64
EMB = 25
READ = 2
LEVELS = 20
ADIM_MAX = 14
ACT = 56
SEQ = 64
F32 = jnp.float32
BF16 = jnp.bfloat16
DP = ("z", "y", "c")
norm_eps = 1e-05


def sent_to_all(x, axis):
    copies = jnp.broadcast_to(x, (lax.axis_size(axis), *x.shape))
    return lax.all_to_all(copies, axis, split_axis=0, concat_axis=0, tiled=True)


def gather_rows(x, axis):
    pieces = sent_to_all(x, axis)
    return pieces.reshape(-1, *x.shape[1:])


def summed_on_arrival(x, axis):
    pieces = x.reshape(lax.axis_size(axis), -1, x.shape[1])
    arrived = lax.all_to_all(pieces, axis, split_axis=0, concat_axis=0, tiled=True)
    return arrived.astype(F32).sum(axis=0)


def summed_for_all(x, axis):
    return sent_to_all(x, axis).astype(F32).sum(axis=0)


def gather_turned(arrays, axis, dims):
    turned = [jnp.moveaxis(a, dim, 0) for a, dim in zip(arrays, dims)]
    widths = [t[0].size for t in turned]
    both = jnp.concatenate([t.reshape(-1, w) for t, w in zip(turned, widths)], axis=1)
    whole = lax.all_gather(both, axis, axis=0, tiled=True)
    pieces = jnp.split(whole, [sum(widths[:k]) for k in range(1, len(widths))], axis=1)
    return tuple(
        (
            jnp.moveaxis(b.reshape(-1, *t.shape[1:]), 0, dim)
            for b, t, dim in zip(pieces, turned, dims)
        )
    )


def normalize(values, scale_gain):
    center = values - jnp.mean(values, axis=-1, keepdims=True)
    spread = jnp.mean(center * center, axis=-1, keepdims=True)
    return center * lax.rsqrt(spread + norm_eps) * scale_gain


def mm(a, b):
    return jnp.dot(a, b, preferred_element_type=F32)


def allowed_keys(observed):
    length = observed.shape[1]
    position = jnp.arange(length)
    visible = (observed == 1) & (position < length - READ)[None, :]
    itself = position[:, None] == position[None, :]
    return visible[:, None, :] | itself[None, :, :]


def attend(queries, key_rows, value_rows, allowed):
    scores = jnp.einsum(
        "sqhd,skhd->shqk", queries, key_rows, preferred_element_type=F32
    ) * HDIM ** (-0.5)
    weights = jnp.where(allowed[:, None, :, :], jnp.exp(scores), 0.0)
    shares = (weights / jnp.sum(weights, axis=-1, keepdims=True)).astype(BF16)
    context = jnp.einsum("shqk,skhd->sqhd", shares, value_rows, preferred_element_type=F32)
    return context.astype(BF16)


def plan():
    steps_up = (jnp.arange(LEVELS, dtype=F32) + 1.0) / LEVELS
    anchor = math.cos(0.008 / 1.008 * math.pi / 2) ** 2
    return jnp.cos((steps_up + 0.008) / 1.008 * (math.pi / 2)) ** 2 / anchor


def noisy_pair(level_ids, clean, noise_draw, table):
    picked = (level_ids[..., None] == jnp.arange(LEVELS)).astype(F32)
    kept = jnp.sum(picked * table, axis=-1)[..., None]
    mixed = jnp.sqrt(kept) * clean.astype(F32) + jnp.sqrt(1.0 - kept) * noise_draw.astype(F32)
    return mixed.astype(BF16)


def tail(first, target, weight_mask, inner_weight, outer_weight, final_weight):
    active = jax.nn.silu(first).astype(BF16)
    inner = jnp.dot(active, inner_weight, preferred_element_type=F32)
    second = jax.nn.silu(inner).astype(BF16)
    hidden = first + jnp.dot(second, outer_weight, preferred_element_type=F32)
    third = jax.nn.silu(hidden).astype(BF16)
    predicted = jnp.dot(third, final_weight, preferred_element_type=F32)
    differ = predicted - target
    return 0.5 * jnp.sum(weight_mask * differ * differ)


def head_grads(first, inner_weight, outer_weight, final_weight, target, weight_mask):

    def head_loss(first_in, inner_in, outer_in, final_in):
        return tail(first_in, target, weight_mask, inner_in, outer_in, final_in)

    loss_value, pullback = jax.vjp(head_loss, first, inner_weight, outer_weight, final_weight)
    return pullback(jnp.ones((), F32))


def on_device(
    tokens,
    obs_mask,
    norm_gains,
    attn_in,
    attn_out,
    mlp_in,
    mlp_out,
    embodiment,
    levels,
    actions,
    noise,
    action_dims,
    head_read,
    head_act,
    time_table,
    block_in,
    block_out,
    head_out,
):
    width = attn_in.shape[3]
    heads = width // HDIM
    peers = lax.axis_size(DP)
    my_model = lax.axis_index("mp")
    my_owner = lax.axis_index(DP)
    owners = embodiment[:, 0]
    place = (jnp.arange(peers)[:, None] == owners[None, :]).astype(BF16)
    noisy = noisy_pair(levels, actions, noise, plan())
    marks = (levels + 1).astype(BF16)[..., None]
    early = jnp.concatenate([noisy, noise, marks, jnp.zeros((*levels.shape, 15), BF16)], axis=-1)
    sent = jnp.einsum("es,srf->erf", place, early, preferred_element_type=F32).astype(BF16)
    got = lax.all_to_all(sent, DP, split_axis=0, concat_axis=0, tiled=True)
    got = got.reshape(peers * READ, 128)

    def weights_of(layer):
        return gather_turned(
            (attn_in[layer], attn_out[layer], mlp_in[layer], mlp_out[layer]), DP, (1, 1, 0, 1)
        )

    residual = tokens.astype(F32)
    normed = normalize(residual, norm_gains[0]).astype(BF16)
    gathered = gather_rows(normed, "mp")
    mask_group = gather_rows(obs_mask, "mp")
    samples = mask_group.shape[0]
    allowed = allowed_keys(mask_group)
    qkv_weight, out_weight, up_weight, down_weight = weights_of(0)
    projected = jnp.einsum("td,jdc->jtc", gathered, qkv_weight, preferred_element_type=F32)
    projected = projected.astype(BF16).reshape(3, samples, SEQ, heads, HDIM)
    context = attend(projected[0], projected[1], projected[2], allowed).reshape(-1, width)
    residual = residual + summed_on_arrival(mm(context, out_weight).astype(BF16), "mp")
    normed = normalize(residual, norm_gains[1]).astype(BF16)
    gathered = gather_rows(normed, "mp")
    hidden = jax.nn.gelu(mm(gathered, up_weight), approximate=True).astype(BF16)
    residual = residual + summed_on_arrival(mm(hidden, down_weight).astype(BF16), "mp")
    whole = gather_rows(residual.astype(BF16), "mp").astype(F32)
    qkv_weight, out_weight, up_weight, down_weight = weights_of(1)
    normed = normalize(whole, norm_gains[2]).astype(BF16)
    last = slice(SEQ - READ, SEQ)
    ending = whole.reshape(samples, SEQ, D)[:, last].reshape(-1, D)
    normed_end = normed.reshape(samples, SEQ, D)[:, last].reshape(-1, D)
    queries = mm(normed_end, qkv_weight[0]).astype(BF16).reshape(samples, READ, heads, HDIM)
    key_rows = mm(normed, qkv_weight[1]).astype(BF16).reshape(samples, SEQ, heads, HDIM)
    value_rows = mm(normed, qkv_weight[2]).astype(BF16).reshape(samples, SEQ, heads, HDIM)
    context = attend(queries, key_rows, value_rows, allowed[:, last]).reshape(-1, width)
    ending = ending + summed_for_all(mm(context, out_weight).astype(BF16), "mp")
    normed = normalize(ending, norm_gains[3]).astype(BF16)
    hidden = jax.nn.gelu(mm(normed, up_weight), approximate=True).astype(BF16)
    ending = ending + summed_for_all(mm(hidden, down_weight).astype(BF16), "mp")
    readouts = normalize(ending, norm_gains[4]).astype(BF16).reshape(samples, READ * D)
    send = mm(place, readouts).astype(BF16)
    features = lax.all_to_all(send, DP, split_axis=0, concat_axis=0, tiled=True)
    features = features.reshape(peers * READ, D)
    head_noisy = got[:, :ACT]
    head_target = got[:, ACT : 2 * ACT].astype(F32)
    head_level = got[:, 2 * ACT].astype(jnp.int32) - 1
    onehot = (head_level[:, None] == jnp.arange(LEVELS)).astype(BF16)
    dims_here = jnp.sum(jnp.where(jnp.arange(EMB) == my_owner, action_dims, 0))
    column = jnp.arange(ACT) % ADIM_MAX
    weight_mask = (head_level >= 0).astype(F32)[:, None] * (column < dims_here).astype(F32)[None, :]
    others = mm(head_noisy, head_act[0]) + mm(onehot, time_table[0])
    first = mm(features, head_read[0]) + others
    grad_first, grad_inner, grad_outer, grad_final = head_grads(
        first,
        block_in[0].astype(F32),
        block_out[0].astype(F32),
        head_out[0].astype(F32),
        head_target,
        weight_mask,
    )
    grad_bf = grad_first.astype(BF16)
    backward = jnp.einsum("nc,dc->nd", grad_bf, head_read[0], preferred_element_type=F32)
    backward = backward.astype(BF16).reshape(peers, READ * D)
    arrived = lax.all_to_all(backward, DP, split_axis=0, concat_axis=0, tiled=True)
    mine = samples // 4
    own_place = lax.dynamic_slice_in_dim(place, my_model * mine, mine, 1)
    arrived = jnp.einsum("es,ef->sf", own_place, arrived, preferred_element_type=F32)
    arrived = arrived.astype(BF16).reshape(mine, READ, D)
    part = lax.dynamic_slice_in_dim(features, my_model * width, width, 1)
    grad_read = jnp.einsum("nd,nc->dc", part, grad_bf, preferred_element_type=F32)
    grad_act = jnp.einsum("na,nc->ac", head_noisy, grad_bf, preferred_element_type=F32)
    grad_time = jnp.einsum("nl,nc->lc", onehot, grad_bf, preferred_element_type=F32)
    return (
        arrived,
        grad_read[None],
        grad_act[None],
        grad_time[None],
        grad_inner[None],
        grad_outer[None],
        grad_final[None],
    )


def solution(mesh):
    fine = Mesh(mesh.devices.reshape(8, 4, 2, 4), ("z", "y", "c", "mp"))
    both = (*DP, "mp")
    placed = (
        P(both, None),
        P(both, None),
        P(),
        P(None, None, DP, "mp"),
        P(None, "mp", DP),
        P(None, DP, "mp"),
        P(None, "mp", DP),
        P(DP, None),
        P(DP, None),
        P(DP, None, None),
        P(DP, None, None),
        P(),
        P(DP, None, None),
        P(DP, None, None),
        P(DP, None, None),
        P(DP, None, None),
        P(DP, None, None),
        P(DP, None, None),
    )
    return jax.shard_map(
        on_device,
        mesh=fine,
        in_specs=placed,
        out_specs=(
            P(both, None, None),
            P(DP, "mp", None),
            P(DP, None, None),
            P(DP, None, None),
            P(DP, None, None),
            P(DP, None, None),
            P(DP, None, None),
        ),
        check_vma=False,
    )
```

profile of v0, /device:TPU:1, one launch (start us, length us, event | category | flops | bytes accessed | tf_op | source)
XLA Modules:
  0.0 302.3 jit_solution(15710188673894022588)
XLA Ops:
  7.3 0.8 fusion.153
  8.1 0.9 fusion.152
  9.1 0.9 fusion.151
  10.0 0.9 fusion.150
  11.0 0.7 concatenate.10
  11.8 0.7 reshape.374
  12.4 4.8 %all-to-all-start.2 = ((s32[4,1,192]{2,1,0:T(1,128)}), s32[4,1,192]{2,1,0:T(1,128)S(1)}, u32[]{:S(2)}, u32[]{:S(2)}) async-start(s32[4,1,192]{2,1,0:T(1,128)} %reshape.374), calls=%async_computation.2 | async-start | bytes 8192 | tf_op jit(solution)/shard_map/all_to_all | solution.py:23
  17.4 0.7 concatenate.11
  18.8 2.6 all-to-all-done.2
  21.4 1.1 broadcast_in_dim.107
  22.5 3.5 %all-to-all-start.1 = ((bf16[4,192,768]{2,1,0:T(8,128)(2,1)}), bf16[4,192,768]{2,1,0:T(8,128)(2,1)S(1)}, u32[]{:S(2)}, u32[]{:S(2)}) async-start(bf16[4,192,768]{2,1,0:T(8,128)(2,1)} %broadcast_in_dim.107), calls=%async_computation.1 | async-start | bytes 2359296 | tf_op jit(solution)/shard_map/all_to_all | solution.py:23
  27.6 67.6 %all-gather.5.cloned.1.call-done = bf16[64,12,2304]{2,1,0:T(8,128)(2,1)} async-done(((bf16[1,12,2304]{2,1,0:T(8,128)(2,1)}), bf16[64,12,2304]{2,1,0:T(8,128)(2,1)}) %all-gather.5.cloned.1.call-update) | async-done | bytes 3538960 | tf_op jit(solution)/shard_map/all_gather | solution.py:45
  95.2 6.4 %reshape.361 = bf16[768,2304]{1,0:T(8,128)(2,1)} reshape(bf16[64,12,2304]{2,1,0:T(8,128)(2,1)} %all-gather.5.cloned.1.call-done) | data formatting | bytes 7077888
  101.6 1.2 slice-done.1
  102.8 1.3 copy.215
  104.1 2.1 fusion.11
  107.2 1.4 squeeze.67
  108.5 2.6 fusion.10
  111.2 2.1 fusion.12
  114.2 1.8 convolution_convert_fusion.3
  115.9 19.9 %all_to_all.67 = bf16[4,192,768]{2,1,0:T(8,128)(2,1)S(1)} all-to-all(bf16[4,192,768]{2,1,0:T(8,128)(2,1)S(1)} %bitcast.164), channel_id=1, replica_groups=mesh['z'=8,'y'=4,'c'=2,'mp'=4] {'mp'}, dimensions={0} | all-to-all | bytes 2359296 | tf_op jit(solution)/shard_map/all_to_all | solution.py:33
  136.6 17.3 %all_to_all.68 = bf16[4,192,768]{2,1,0:T(8,128)(2,1)S(1)} all-to-all(bf16[4,192,768]{2,1,0:T(8,128)(2,1)S(1)} %broadcast_in_dim.111), channel_id=1, replica_groups=mesh['z'=8,'y'=4,'c'=2,'mp'=4] {'mp'}, dimensions={0} | all-to-all | bytes 2359296 | tf_op jit(solution)/shard_map/all_to_all | solution.py:23
  153.9 4.9 %convolution_convert_fusion.2 = bf16[768,768]{1,0:T(8,128)(2,1)} fusion(bf16[768,2304]{1,0:T(8,128)(2,1)} %reshape.361, bf16[768,768]{1,0:T(8,128)(2,1)S(1)} %bitcast.177), kind=kOutput, calls=%fused_computation.17 | convolution fusion | flops 1817837568 | bytes 4718592 | tf_op jit(solution)/shard_map/dot_general | solution.py:62
  158.8 3.7 %all-to-all-start.5 = ((bf16[4,192,768]{2,1,0:T(8,128)(2,1)}), bf16[4,192,768]{2,1,0:T(8,128)(2,1)S(1)}, u32[]{:S(2)}, u32[]{:S(2)}) async-start(bf16[4,192,768]{2,1,0:T(8,128)(2,1)} %bitcast.174), calls=%async_computation.5 | async-start | bytes 2359296 | tf_op jit(solution)/shard_map/all_to_all | solution.py:33
  162.9 13.6 %all-to-all-done.5 = bf16[4,192,768]{2,1,0:T(8,128)(2,1)S(1)} async-done(((bf16[4,192,768]{2,1,0:T(8,128)(2,1)}), bf16[4,192,768]{2,1,0:T(8,128)(2,1)S(1)}, u32[]{:S(2)}, u32[]{:S(2)}) %all-to-all-start.5) | async-done | bytes 1179680 | tf_op jit(solution)/shard_map/all_to_all | solution.py:33
  176.7 1.2 broadcast_in_dim.112
  177.9 3.9 %all-to-all-start.6 = ((bf16[4,192,768]{2,1,0:T(8,128)(2,1)}), bf16[4,192,768]{2,1,0:T(8,128)(2,1)S(1)}, u32[]{:S(2)}, u32[]{:S(2)}) async-start(bf16[4,192,768]{2,1,0:T(8,128)(2,1)} %broadcast_in_dim.112), calls=%async_computation.6 | async-start | bytes 2359296 | tf_op jit(solution)/shard_map/all_to_all | solution.py:23
  184.7 6.4 %reshape.363 = bf16[768,2304]{1,0:T(8,128)(2,1)} reshape(bf16[64,12,2304]{2,1,0:T(8,128)(2,1)} %all-gather.7.cloned.1.call-done) | data formatting | bytes 7077888
  191.2 1.2 slice-done
  193.0 1.5 all-to-all-done.6
  195.8 1.3 convolution_convert_fusion.6
  197.1 1.3 convolution_convert_fusion.7
  198.5 1.4 reshape.350
  200.0 2.3 reshape.353
  202.5 1.4 copy-done.2
  204.4 1.4 fusion.36
  206.4 1.4 convolution_convert_fusion.12
  207.8 0.7 broadcast_in_dim.115
  208.5 3.3 %all-to-all-start.7 = ((bf16[4,24,768]{2,1,0:T(8,128)(2,1)}), bf16[4,24,768]{2,1,0:T(8,128)(2,1)S(1)}, u32[]{:S(2)}, u32[]{:S(2)}) async-start(bf16[4,24,768]{2,1,0:T(8,128)(2,1)} %broadcast_in_dim.115), calls=%async_computation.7 | async-start | bytes 294912 | tf_op jit(solution)/shard_map/all_to_all | solution.py:23
  212.6 4.1 %all-to-all-done.7 = bf16[4,24,768]{2,1,0:T(8,128)(2,1)S(1)} async-done(((bf16[4,24,768]{2,1,0:T(8,128)(2,1)}), bf16[4,24,768]{2,1,0:T(8,128)(2,1)S(1)}, u32[]{:S(2)}, u32[]{:S(2)}) %all-to-all-start.7) | async-done | bytes 147488 | tf_op jit(solution)/shard_map/all_to_all | solution.py:23
  216.7 11.9 %all-to-all-start = ((bf16[64,2,128]{2,1,0:T(2,128)(2,1)}), bf16[64,2,128]{2,1,0:T(2,128)(2,1)S(1)}, u32[]{:S(2)}, u32[]{:S(2)}) async-start(bf16[64,2,128]{2,1,0:T(2,128)(2,1)} %copy.209), calls=%async_computation | async-start | bytes 65536 | tf_op jit(solution)/shard_map/all_to_all | solution.py:147
  228.6 1.1 fusion.146
  229.8 1.2 multiply_reduce_fusion.3
  231.1 2.4 fusion.32
  233.4 4.5 %all-to-all-done = bf16[64,2,128]{2,1,0:T(2,128)(2,1)S(1)} async-done(((bf16[64,2,128]{2,1,0:T(2,128)(2,1)}), bf16[64,2,128]{2,1,0:T(2,128)(2,1)S(1)}, u32[]{:S(2)}, u32[]{:S(2)}) %all-to-all-start) | async-done | bytes 32800 | tf_op jit(solution)/shard_map/all_to_all | solution.py:147
  237.9 0.7 broadcast_in_dim.116
  238.6 3.3 %all-to-all-start.8 = ((bf16[4,24,768]{2,1,0:T(8,128)(2,1)}), bf16[4,24,768]{2,1,0:T(8,128)(2,1)S(1)}, u32[]{:S(2)}, u32[]{:S(2)}) async-start(bf16[4,24,768]{2,1,0:T(8,128)(2,1)} %broadcast_in_dim.116), calls=%async_computation.8 | async-start | bytes 294912 | tf_op jit(solution)/shard_map/all_to_all | solution.py:23
  242.2 4.6 %all-to-all-done.8 = bf16[4,24,768]{2,1,0:T(8,128)(2,1)S(1)} async-done(((bf16[4,24,768]{2,1,0:T(8,128)(2,1)}), bf16[4,24,768]{2,1,0:T(8,128)(2,1)S(1)}, u32[]{:S(2)}, u32[]{:S(2)}) %all-to-all-start.8) | async-done | bytes 147488 | tf_op jit(solution)/shard_map/all_to_all | solution.py:23
  246.9 1.1 fusion.147
  249.4 0.7 reduce.22
  250.1 0.7 reshape.376
  250.8 7.0 %all-to-all-start.9 = ((bf16[64,2,768]{2,1,0:T(2,128)(2,1)}), bf16[64,2,768]{2,1,0:T(2,128)(2,1)S(1)}, u32[]{:S(2)}, u32[]{:S(2)}) async-start(bf16[64,2,768]{2,1,0:T(2,128)(2,1)} %reshape.376), calls=%async_computation.9 | async-start | bytes 393216 | tf_op jit(solution)/shard_map/all_to_all | solution.py:186
  258.7 11.2 %all-to-all-done.9 = bf16[64,2,768]{2,1,0:T(2,128)(2,1)S(1)} async-done(((bf16[64,2,768]{2,1,0:T(2,128)(2,1)}), bf16[64,2,768]{2,1,0:T(2,128)(2,1)S(1)}, u32[]{:S(2)}, u32[]{:S(2)}) %all-to-all-start.9) | async-done | bytes 196640 | tf_op jit(solution)/shard_map/all_to_all | solution.py:186
  270.0 1.1 reduce.12
  273.6 1.0 convolution_bitcast_fusion.2
  274.7 1.8 reduce.23
  276.5 0.7 reshape.378
  277.2 4.5 %all-to-all-start.10 = ((bf16[64,2,768]{2,1,0:T(2,128)(2,1)}), bf16[64,2,768]{2,1,0:T(2,128)(2,1)S(1)}, u32[]{:S(2)}, u32[]{:S(2)}) async-start(bf16[64,2,768]{2,1,0:T(2,128)(2,1)} %reshape.378), calls=%async_computation.10 | async-start | bytes 393216 | tf_op jit(solution)/shard_map/all_to_all | solution.py:208
  281.7 0.8 convolution_bitcast_fusion.3
  283.0 0.8 convolution_bitcast_fusion.4
  283.8 0.9 convolution_bitcast_fusion.1
  284.8 0.9 convolution_bitcast_fusion
  285.7 8.1 %all-to-all-done.10 = bf16[64,2,768]{2,1,0:T(2,128)(2,1)S(1)} async-done(((bf16[64,2,768]{2,1,0:T(2,128)(2,1)}), bf16[64,2,768]{2,1,0:T(2,128)(2,1)S(1)}, u32[]{:S(2)}, u32[]{:S(2)}) %all-to-all-start.10) | async-done | bytes 196640 | tf_op jit(solution)/shard_map/all_to_all | solution.py:208
  293.9 0.8 convolution_convert_fusion.1
  (161 shorter events, 19.2 us)
Async XLA Ops:
  7.2 264.1 %copy-start = (bf16[1,768,256]{2,1,0:T(8,128)(2,1)S(1)}, bf16[1,768,256]{2,1,0:T(8,128)(2,1)}, u32[]{:S(2)}) copy-start(bf16[1,768,256]{2,1,0:T(8,128)(2,1)} %param.30) | copy-start | bytes 1179652
  7.2 4.6 %copy-start.10 = (s32[3,64]{1,0:T(4,128)S(1)}, s32[3,64]{1,0:T(4,128)}, u32[]{:S(2)}) copy-start(s32[3,64]{1,0:T(4,128)} %param.19) | copy-start | bytes 2308
  7.2 10.9 %copy-start.1 = (bf16[192,768]{1,0:T(8,128)(2,1)S(1)}, bf16[192,768]{1,0:T(8,128)(2,1)}, u32[]{:S(2)}) copy-start(bf16[192,768]{1,0:T(8,128)(2,1)} %param.18) | copy-start | bytes 884740
  7.2 11.3 %copy-start.6 = (f32[5,768]{1,0:T(8,128)S(1)}, f32[5,768]{1,0:T(8,128)}, u32[]{:S(2)}) copy-start(f32[5,768]{1,0:T(8,128)} %param.20) | copy-start | bytes 46084
  7.2 88.0 %all-gather.5.cloned.1.call-start = ((), (), s32[]{:S(2)}) async-start(), calls=%async_computation.11 | async-start | bytes 4792320 | tf_op jit(solution)/shard_map/all_gather | solution.py:45
  12.4 9.0 %all-to-all-start.2 = ((s32[4,1,192]{2,1,0:T(1,128)}), s32[4,1,192]{2,1,0:T(1,128)S(1)}, u32[]{:S(2)}, u32[]{:S(2)}) async-start(s32[4,1,192]{2,1,0:T(1,128)} %reshape.374), calls=%async_computation.2 | async-start | bytes 8192 | tf_op jit(solution)/shard_map/all_to_all | solution.py:23
  17.3 167.5 %all-gather.7.cloned.1.call-start = ((), (), s32[]{:S(2)}) async-start(), calls=%async_computation.12 | async-start | bytes 4792320 | tf_op jit(solution)/shard_map/all_gather | solution.py:45
  22.5 81.6 %all-to-all-start.1 = ((bf16[4,192,768]{2,1,0:T(8,128)(2,1)}), bf16[4,192,768]{2,1,0:T(8,128)(2,1)S(1)}, u32[]{:S(2)}, u32[]{:S(2)}) async-start(bf16[4,192,768]{2,1,0:T(8,128)(2,1)} %broadcast_in_dim.107), calls=%async_computation.1 | async-start | bytes 2359296 | tf_op jit(solution)/shard_map/all_to_all | solution.py:23
  101.6 1.2 slice-start.1
  158.8 3.7 %copy-start.11 = (s32[12,2]{0,1:T(2,128)S(1)}, s32[12,2]{0,1:T(2,128)}, u32[]{:S(2)}) copy-start(s32[12,2]{0,1:T(2,128)} %param.26) | copy-start | bytes 292
  158.8 17.7 %all-to-all-start.5 = ((bf16[4,192,768]{2,1,0:T(8,128)(2,1)}), bf16[4,192,768]{2,1,0:T(8,128)(2,1)S(1)}, u32[]{:S(2)}, u32[]{:S(2)}) async-start(bf16[4,192,768]{2,1,0:T(8,128)(2,1)} %bitcast.174), calls=%async_computation.5 | async-start | bytes 2359296 | tf_op jit(solution)/shard_map/all_to_all | solution.py:33
  177.9 4.0 %copy-start.4 = (bf16[12,2,56]{2,1,0:T(2,128)(2,1)S(1)}, bf16[12,2,56]{2,1,0:T(2,128)(2,1)}, u32[]{:S(2)}) copy-start(bf16[12,2,56]{2,1,0:T(2,128)(2,1)} %param.28) | copy-start | bytes 8068
  177.9 4.1 %copy-start.7 = (bf16[12,2,56]{2,1,0:T(2,128)(2,1)S(1)}, bf16[12,2,56]{2,1,0:T(2,128)(2,1)}, u32[]{:S(2)}) copy-start(bf16[12,2,56]{2,1,0:T(2,128)(2,1)} %param.27) | copy-start | bytes 8068
  177.9 4.2 %copy-start.8 = (s32[12,1]{0,1:T(1,128)S(1)}, s32[12,1]{0,1:T(1,128)}, u32[]{:S(2)}) copy-start(s32[12,1]{0,1:T(1,128)} %param.25) | copy-start | bytes 148
  177.9 5.1 %copy-start.15 = (s32[25]{0:T(128)S(1)}, s32[25]{0:T(128)}, u32[]{:S(2)}) copy-start(s32[25]{0:T(128)} %param.29) | copy-start | bytes 304
  177.9 16.5 %all-to-all-start.6 = ((bf16[4,192,768]{2,1,0:T(8,128)(2,1)}), bf16[4,192,768]{2,1,0:T(8,128)(2,1)S(1)}, u32[]{:S(2)}, u32[]{:S(2)}) async-start(bf16[4,192,768]{2,1,0:T(8,128)(2,1)} %broadcast_in_dim.112), calls=%async_computation.6 | async-start | bytes 2359296 | tf_op jit(solution)/shard_map/all_to_all | solution.py:23
  191.2 1.2 slice-start
  202.5 1.4 copy-start.2
  208.5 8.2 %all-to-all-start.7 = ((bf16[4,24,768]{2,1,0:T(8,128)(2,1)}), bf16[4,24,768]{2,1,0:T(8,128)(2,1)S(1)}, u32[]{:S(2)}, u32[]{:S(2)}) async-start(bf16[4,24,768]{2,1,0:T(8,128)(2,1)} %broadcast_in_dim.115), calls=%async_computation.7 | async-start | bytes 294912 | tf_op jit(solution)/shard_map/all_to_all | solution.py:23
  216.7 21.2 %all-to-all-start = ((bf16[64,2,128]{2,1,0:T(2,128)(2,1)}), bf16[64,2,128]{2,1,0:T(2,128)(2,1)S(1)}, u32[]{:S(2)}, u32[]{:S(2)}) async-start(bf16[64,2,128]{2,1,0:T(2,128)(2,1)} %copy.209), calls=%async_computation | async-start | bytes 65536 | tf_op jit(solution)/shard_map/all_to_all | solution.py:147
  231.1 10.8 %copy-start.3 = (bf16[1,56,256]{2,1,0:T(8,128)(2,1)S(1)}, bf16[1,56,256]{2,1,0:T(8,128)(2,1)}, u32[]{:S(2)}) copy-start(bf16[1,56,256]{2,1,0:T(8,128)(2,1)} %param.31) | copy-start | bytes 86020
  238.6 8.2 %all-to-all-start.8 = ((bf16[4,24,768]{2,1,0:T(8,128)(2,1)}), bf16[4,24,768]{2,1,0:T(8,128)(2,1)S(1)}, u32[]{:S(2)}, u32[]{:S(2)}) async-start(bf16[4,24,768]{2,1,0:T(8,128)(2,1)} %broadcast_in_dim.116), calls=%async_computation.8 | async-start | bytes 294912 | tf_op jit(solution)/shard_map/all_to_all | solution.py:23
  242.1 6.5 %copy-start.9 = (s32[12,1]{0,1:T(1,128)S(1)}, s32[12,1]{0,1:T(1,128)}, u32[]{:S(2)}) copy-start(s32[12,1]{0,1:T(1,128)} %param.25) | copy-start | bytes 148
  248.5 10.0 %copy-start.5 = (bf16[1,20,256]{2,1,0:T(8,128)(2,1)S(1)}, bf16[1,20,256]{2,1,0:T(8,128)(2,1)}, u32[]{:S(2)}) copy-start(bf16[1,20,256]{2,1,0:T(8,128)(2,1)} %param.32) | copy-start | bytes 30724
  250.8 19.0 %all-to-all-start.9 = ((bf16[64,2,768]{2,1,0:T(2,128)(2,1)}), bf16[64,2,768]{2,1,0:T(2,128)(2,1)S(1)}, u32[]{:S(2)}, u32[]{:S(2)}) async-start(bf16[64,2,768]{2,1,0:T(2,128)(2,1)} %reshape.376), calls=%async_computation.9 | async-start | bytes 393216 | tf_op jit(solution)/shard_map/all_to_all | solution.py:186
  258.7 12.8 %copy-start.13 = (bf16[1,256,256]{2,1,0:T(8,128)(2,1)S(1)}, bf16[1,256,256]{2,1,0:T(8,128)(2,1)}, u32[]{:S(2)}) copy-start(bf16[1,256,256]{2,1,0:T(8,128)(2,1)} %param.33) | copy-start | bytes 393220
  270.0 1.7 copy-start.12
  271.5 0.8 copy-start.14
  277.2 16.6 %all-to-all-start.10 = ((bf16[64,2,768]{2,1,0:T(2,128)(2,1)}), bf16[64,2,768]{2,1,0:T(2,128)(2,1)S(1)}, u32[]{:S(2)}, u32[]{:S(2)}) async-start(bf16[64,2,768]{2,1,0:T(2,128)(2,1)} %reshape.378), calls=%async_computation.10 | async-start | bytes 393216 | tf_op jit(solution)/shard_map/all_to_all | solution.py:208
Sparse Core Ops, SparseCore 0:
  11.9 83.2 all-gather.4
  98.5 76.5 all-gather.6
where the time goes:
time: 304 us; the launch traced here: 302 us
  waiting for transfers between devices  118 us (39%)
  starting transfers between devices  45.9 us (15%)
  local copies, waits for them, and re-layouts  42.7 us (14%)
  blocking collectives  37.2 us (12%)
  matrix products  29.9 us (10%)
  between operations  14.9 us (5%)
  other arithmetic  13.7 us (5%)
    all_gather x2, waiting for transfers between devices, gather_turned(): whole = lax.all_gather(both, axis, axis=0, tiled=True)  67.6 us
    all_to_all x1, blocking collectives, summed_on_arrival(): lax.all_to_all(pieces, axis, split_axis=0, concat_axis=0, tiled=True)  19.9 us
    all_to_all x5, starting transfers between devices, sent_to_all(): return lax.all_to_all(copies, axis, split_axis=0, concat_axis=0, tiled=True)  18.9 us
    unnamed x50, local copies, waits for them, and re-layouts  18.1 us
    all_to_all x1, blocking collectives, sent_to_all(): return lax.all_to_all(copies, axis, split_axis=0, concat_axis=0, tiled=True)  17.3 us
    dot_general x11, matrix products, mm(): return jnp.dot(a, b, preferred_element_type=F32)  14 us
    all_to_all x1, waiting for transfers between devices, summed_on_arrival(): lax.all_to_all(pieces, axis, split_axis=0, concat_axis=0, tiled=True)  13.6 us
    all_to_all x5, waiting for transfers between devices, sent_to_all(): return lax.all_to_all(copies, axis, split_axis=0, concat_axis=0, tiled=True)  12.9 us
  transfers between devices with their start and end apart: 11, of which 9 were waited for; matrix products, arithmetic and copies ran while one was open for 17% of the time, Pallas kernels for 0%

commit v1 on v0

--- a/solution.py
+++ b/solution.py
@@ -18,6 +18,13 @@
 norm_eps = 1e-05
 
 
+def all_by_exchange(x, axis, dim):
+    n_dev = lax.axis_size(axis)
+    blocks = jnp.stack([x for _ in range(n_dev)])
+    blocks = lax.all_to_all(blocks, axis, split_axis=0, concat_axis=0)
+    return jnp.concatenate(blocks, axis=dim)
+
+
 def sent_to_all(x, axis):
     copies = jnp.broadcast_to(x, (lax.axis_size(axis), *x.shape))
     return lax.all_to_all(copies, axis, split_axis=0, concat_axis=0, tiled=True)
@@ -42,7 +49,7 @@
     turned = [jnp.moveaxis(a, dim, 0) for a, dim in zip(arrays, dims)]
     widths = [t[0].size for t in turned]
     both = jnp.concatenate([t.reshape(-1, w) for t, w in zip(turned, widths)], axis=1)
-    whole = lax.all_gather(both, axis, axis=0, tiled=True)
+    whole = all_by_exchange(both, axis, 0)
     pieces = jnp.split(whole, [sum(widths[:k]) for k in range(1, len(widths))], axis=1)
     return tuple(
         (

time: 304 us -> 462 us (1.52)
  waiting for transfers between devices: 118 us -> 259 us
  starting transfers between devices: 45.9 us -> 81.2 us
  between operations: 14.9 us -> 1.47 us
  blocking collectives: 37.2 us -> 29.4 us
  local copies, waits for them, and re-layouts: 42.7 us -> 48.6 us
    all_to_all x0 -> x2, waiting for transfers between devices: none -> 209 us  [all_by_exchange(): blocks = lax.all_to_all(blocks, axis, split_axis=0, concat_axis=0)]
    all_gather x2 -> x0, waiting for transfers between devices: 67.6 us -> none  [gather_turned(): whole = lax.all_gather(both, axis, axis=0, tiled=True)]
    all_to_all x0 -> x2, starting transfers between devices: none -> 35.8 us  [all_by_exchange(): blocks = lax.all_to_all(blocks, axis, split_axis=0, concat_axis=0)]
    unnamed x50 -> x58, local copies, waits for them, and re-layouts: 18.1 us -> 5.14 us
    reshape x0 -> x2, local copies, waits for them, and re-layouts: none -> 12.8 us  [all_by_exchange(): return jnp.concatenate(blocks, axis=dim)]
    another operation x0 -> x2, local copies, waits for them, and re-layouts: none -> 4.95 us  [all_by_exchange(): blocks = jnp.stack([x for _ in range(n_dev)])]
    all_to_all x1, blocking collectives: 19.9 us -> 15.1 us  [summed_on_arrival(): lax.all_to_all(pieces, axis, split_axis=0, concat_axis=0, tiled=True)]
  transfers between devices with their start and end apart: 11 -> 11, of which waited for: 9 -> 10; matrix products, arithmetic and copies ran while one was open for 17% -> 8% of each run, Pallas kernels for 0% -> 0%
where the time goes in v1:
time: 462 us; the launch traced here: 460 us
  waiting for transfers between devices  259 us (56%)
  starting transfers between devices  81.2 us (18%)
  local copies, waits for them, and re-layouts  48.6 us (11%)
  blocking collectives  29.4 us (6%)
  matrix products  26.8 us (6%)
  other arithmetic  13.2 us (3%)
    all_to_all x2, waiting for transfers between devices, all_by_exchange(): blocks = lax.all_to_all(blocks, axis, split_axis=0, concat_axis=0)  209 us
    all_to_all x2, starting transfers between devices, all_by_exchange(): blocks = lax.all_to_all(blocks, axis, split_axis=0, concat_axis=0)  35.8 us
    all_to_all x5, starting transfers between devices, sent_to_all(): return lax.all_to_all(copies, axis, split_axis=0, concat_axis=0, tiled=True)  19.7 us
    all_to_all x5, waiting for transfers between devices, sent_to_all(): return lax.all_to_all(copies, axis, split_axis=0, concat_axis=0, tiled=True)  15.7 us
    all_to_all x1, blocking collectives, summed_on_arrival(): lax.all_to_all(pieces, axis, split_axis=0, concat_axis=0, tiled=True)  15.1 us
    all_to_all x1, blocking collectives, sent_to_all(): return lax.all_to_all(copies, axis, split_axis=0, concat_axis=0, tiled=True)  14.3 us
    dot_general x11, matrix products, mm(): return jnp.dot(a, b, preferred_element_type=F32)  13.9 us
    reshape x2, local copies, waits for them, and re-layouts, all_by_exchange(): return jnp.concatenate(blocks, axis=dim)  12.8 us
  transfers between devices with their start and end apart: 11, of which 10 were waited for; matrix products, arithmetic and copies ran while one was open for 8% of the time, Pallas kernels for 0%

profile of v1, /device:TPU:1, one launch (start us, length us, event | category | flops | bytes accessed | tf_op | source)
XLA Modules:
  0.0 460.0 jit_solution(14792417717089599267)
XLA Ops:
  0.6 0.7 broadcast_in_dim.108
  2.1 4.8 %all-to-all-start.3 = ((s32[4,1,192]{2,1,0:T(1,128)}), s32[4,1,192]{2,1,0:T(1,128)S(1)}, u32[]{:S(2)}, u32[]{:S(2)}) async-start(s32[4,1,192]{2,1,0:T(1,128)} %reshape.382), calls=%async_computation.3 | async-start | bytes 8192 | tf_op jit(solution)/shard_map/all_to_all | solution.py:30
  6.9 0.9 fusion.152
  7.8 0.9 fusion.151
  8.7 0.9 fusion.150
  9.6 0.8 fusion.153
  12.5 2.5 stack.4
  15.0 12.9 %all-to-all-start.1 = ((bf16[64,12,2304]{2,1,0:T(8,128)(2,1)}), bf16[64,12,2304]{2,1,0:T(8,128)(2,1)}, u32[]{:S(2)}, u32[]{:S(2)}) async-start(bf16[64,12,2304]{2,1,0:T(8,128)(2,1)} %stack.4), calls=%async_computation.1 | async-start | bytes 9437184 | tf_op jit(solution)/shard_map/all_to_all | solution.py:24
  29.1 104.4 %all-to-all-done.1 = bf16[64,12,2304]{2,1,0:T(8,128)(2,1)} async-done(((bf16[64,12,2304]{2,1,0:T(8,128)(2,1)}), bf16[64,12,2304]{2,1,0:T(8,128)(2,1)}, u32[]{:S(2)}, u32[]{:S(2)}) %all-to-all-start.1) | async-done | bytes 3538976 | tf_op jit(solution)/shard_map/all_to_all | solution.py:24
  133.5 1.2 broadcast_in_dim.107
  134.7 4.5 all-to-all-start.2
  140.7 6.4 %reshape.351 = bf16[768,2304]{1,0:T(8,128)(2,1)} reshape(bf16[64,12,2304]{2,1,0:T(8,128)(2,1)} %all-to-all-done.1) | data formatting | bytes 7077888 | tf_op jit(solution)/shard_map/reshape | solution.py:25
  147.1 1.2 slice-done.1
  148.3 1.3 copy.215
  149.6 3.2 all-to-all-done.2
  152.8 2.0 fusion.11
  155.8 1.4 squeeze.66
  157.2 1.5 fusion.10
  158.7 2.0 fusion.12
  161.6 1.8 convolution_convert_fusion.3
  163.4 15.1 %all_to_all.77 = bf16[4,192,768]{2,1,0:T(8,128)(2,1)S(1)} all-to-all(bf16[4,192,768]{2,1,0:T(8,128)(2,1)S(1)} %bitcast.162), channel_id=1, replica_groups=mesh['z'=8,'y'=4,'c'=2,'mp'=4] {'mp'}, dimensions={0} | all-to-all | bytes 2359296 | tf_op jit(solution)/shard_map/all_to_all | solution.py:40
  179.3 14.3 %all_to_all.78 = bf16[4,192,768]{2,1,0:T(8,128)(2,1)S(1)} all-to-all(bf16[4,192,768]{2,1,0:T(8,128)(2,1)S(1)} %broadcast_in_dim.111), channel_id=1, replica_groups=mesh['z'=8,'y'=4,'c'=2,'mp'=4] {'mp'}, dimensions={0} | all-to-all | bytes 2359296 | tf_op jit(solution)/shard_map/all_to_all | solution.py:30
  193.6 4.8 %convolution_convert_fusion.2 = bf16[768,768]{1,0:T(8,128)(2,1)} fusion(bf16[768,2304]{1,0:T(8,128)(2,1)} %reshape.351, bf16[768,768]{1,0:T(8,128)(2,1)S(1)} %bitcast.175), kind=kOutput, calls=%fused_computation.17 | convolution fusion | flops 1817837568 | bytes 4718592 | tf_op jit(solution)/shard_map/dot_general | solution.py:69
  198.4 3.7 all-to-all-start.6
  202.3 10.5 %all-to-all-done.6 = bf16[4,192,768]{2,1,0:T(8,128)(2,1)S(1)} async-done(((bf16[4,192,768]{2,1,0:T(8,128)(2,1)}), bf16[4,192,768]{2,1,0:T(8,128)(2,1)S(1)}, u32[]{:S(2)}, u32[]{:S(2)}) %all-to-all-start.6) | async-done | bytes 1179680 | tf_op jit(solution)/shard_map/all_to_all | solution.py:40
  212.8 2.5 stack.5
  215.2 22.9 %all-to-all-start.8 = ((bf16[64,12,2304]{2,1,0:T(8,128)(2,1)}), bf16[64,12,2304]{2,1,0:T(8,128)(2,1)}, u32[]{:S(2)}, u32[]{:S(2)}) async-start(bf16[64,12,2304]{2,1,0:T(8,128)(2,1)} %stack.5), calls=%async_computation.8 | async-start | bytes 9437184 | tf_op jit(solution)/shard_map/all_to_all | solution.py:24
  238.8 105.1 %all-to-all-done.8 = bf16[64,12,2304]{2,1,0:T(8,128)(2,1)} async-done(((bf16[64,12,2304]{2,1,0:T(8,128)(2,1)}), bf16[64,12,2304]{2,1,0:T(8,128)(2,1)}, u32[]{:S(2)}, u32[]{:S(2)}) %all-to-all-start.8) | async-done | bytes 3538976 | tf_op jit(solution)/shard_map/all_to_all | solution.py:24
  343.9 1.2 broadcast_in_dim.112
  345.1 3.7 all-to-all-start.7
  351.2 6.4 %reshape.360 = bf16[768,2304]{1,0:T(8,128)(2,1)} reshape(bf16[64,12,2304]{2,1,0:T(8,128)(2,1)} %all-to-all-done.8) | data formatting | bytes 7077888 | tf_op jit(solution)/shard_map/reshape | solution.py:25
  357.6 1.2 slice-done
  359.4 3.7 all-to-all-done.7
  364.5 1.3 convolution_convert_fusion.6
  365.8 1.3 convolution_convert_fusion.7
  367.4 1.3 copy-done.2
  369.1 1.5 reshape.365
  370.6 1.4 reshape.362
  372.9 1.4 convolution_convert_fusion.12
  374.3 0.7 broadcast_in_dim.115
  375.0 3.3 all-to-all-start.9
  379.1 4.1 all-to-all-done.9
  383.2 10.6 %all-to-all-start = ((bf16[64,2,128]{2,1,0:T(2,128)(2,1)}), bf16[64,2,128]{2,1,0:T(2,128)(2,1)S(1)}, u32[]{:S(2)}, u32[]{:S(2)}) async-start(bf16[64,2,128]{2,1,0:T(2,128)(2,1)} %copy.209), calls=%async_computation | async-start | bytes 65536 | tf_op jit(solution)/shard_map/all_to_all | solution.py:154
  393.9 1.1 fusion.146
  395.0 1.1 multiply_reduce_fusion.3
  396.4 2.4 fusion.32
  398.7 4.5 all-to-all-done
  403.8 3.3 all-to-all-start.10
  407.4 4.6 %all-to-all-done.10 = bf16[4,24,768]{2,1,0:T(8,128)(2,1)S(1)} async-done(((bf16[4,24,768]{2,1,0:T(8,128)(2,1)}), bf16[4,24,768]{2,1,0:T(8,128)(2,1)S(1)}, u32[]{:S(2)}, u32[]{:S(2)}) %all-to-all-start.10) | async-done | bytes 147488 | tf_op jit(solution)/shard_map/all_to_all | solution.py:30
  412.2 1.1 fusion.147
  414.7 0.7 reduce.22
  415.4 0.7 reshape.384
  416.1 7.0 %all-to-all-start.11 = ((bf16[64,2,768]{2,1,0:T(2,128)(2,1)}), bf16[64,2,768]{2,1,0:T(2,128)(2,1)S(1)}, u32[]{:S(2)}, u32[]{:S(2)}) async-start(bf16[64,2,768]{2,1,0:T(2,128)(2,1)} %reshape.384), calls=%async_computation.11 | async-start | bytes 393216 | tf_op jit(solution)/shard_map/all_to_all | solution.py:193
  423.9 11.2 %all-to-all-done.11 = bf16[64,2,768]{2,1,0:T(2,128)(2,1)S(1)} async-done(((bf16[64,2,768]{2,1,0:T(2,128)(2,1)}), bf16[64,2,768]{2,1,0:T(2,128)(2,1)S(1)}, u32[]{:S(2)}, u32[]{:S(2)}) %all-to-all-start.11) | async-done | bytes 196640 | tf_op jit(solution)/shard_map/all_to_all | solution.py:193
  435.3 1.1 reduce.12
  438.9 1.0 convolution_bitcast_fusion.2
  439.9 1.8 reduce.23
  441.7 0.7 reshape.386
  442.5 4.5 all-to-all-start.12
  446.9 0.8 convolution_bitcast_fusion.3
  448.3 0.8 convolution_bitcast_fusion.4
  449.1 0.9 convolution_bitcast_fusion.1
  450.1 0.9 convolution_bitcast_fusion
  451.0 8.1 %all-to-all-done.12 = bf16[64,2,768]{2,1,0:T(2,128)(2,1)S(1)} async-done(((bf16[64,2,768]{2,1,0:T(2,128)(2,1)}), bf16[64,2,768]{2,1,0:T(2,128)(2,1)S(1)}, u32[]{:S(2)}, u32[]{:S(2)}) %all-to-all-start.12) | async-done | bytes 196640 | tf_op jit(solution)/shard_map/all_to_all | solution.py:215
  (171 shorter events, 22.9 us)
Async XLA Ops:
  0.6 435.9 %copy-start = (bf16[1,768,256]{2,1,0:T(8,128)(2,1)S(1)}, bf16[1,768,256]{2,1,0:T(8,128)(2,1)}, u32[]{:S(2)}) copy-start(bf16[1,768,256]{2,1,0:T(8,128)(2,1)} %param.30) | copy-start | bytes 1179652
  2.1 10.4 %all-to-all-start.3 = ((s32[4,1,192]{2,1,0:T(1,128)}), s32[4,1,192]{2,1,0:T(1,128)S(1)}, u32[]{:S(2)}, u32[]{:S(2)}) async-start(s32[4,1,192]{2,1,0:T(1,128)} %reshape.382), calls=%async_computation.3 | async-start | bytes 8192 | tf_op jit(solution)/shard_map/all_to_all | solution.py:30
  15.0 12.9 %copy-start.11 = (f32[5,768]{1,0:T(8,128)S(1)}, f32[5,768]{1,0:T(8,128)}, u32[]{:S(2)}) copy-start(f32[5,768]{1,0:T(8,128)} %param.20) | copy-start | bytes 46084
  15.0 13.6 %copy-start.1 = (bf16[192,768]{1,0:T(8,128)(2,1)S(1)}, bf16[192,768]{1,0:T(8,128)(2,1)}, u32[]{:S(2)}) copy-start(bf16[192,768]{1,0:T(8,128)(2,1)} %param.18) | copy-start | bytes 884740
  15.0 118.5 %all-to-all-start.1 = ((bf16[64,12,2304]{2,1,0:T(8,128)(2,1)}), bf16[64,12,2304]{2,1,0:T(8,128)(2,1)}, u32[]{:S(2)}, u32[]{:S(2)}) async-start(bf16[64,12,2304]{2,1,0:T(8,128)(2,1)} %stack.4), calls=%async_computation.1 | async-start | bytes 9437184 | tf_op jit(solution)/shard_map/all_to_all | solution.py:24
  134.7 18.1 %all-to-all-start.2 = ((bf16[4,192,768]{2,1,0:T(8,128)(2,1)}), bf16[4,192,768]{2,1,0:T(8,128)(2,1)S(1)}, u32[]{:S(2)}, u32[]{:S(2)}) async-start(bf16[4,192,768]{2,1,0:T(8,128)(2,1)} %broadcast_in_dim.107), calls=%async_computation.2 | async-start | bytes 2359296 | tf_op jit(solution)/shard_map/all_to_all | solution.py:30
  147.1 1.2 slice-start.1
  157.2 1.5 copy-start.3
  198.4 3.7 copy-start.6
  198.4 3.8 copy-start.4
  198.4 3.8 copy-start.5
  198.4 14.3 %all-to-all-start.6 = ((bf16[4,192,768]{2,1,0:T(8,128)(2,1)}), bf16[4,192,768]{2,1,0:T(8,128)(2,1)S(1)}, u32[]{:S(2)}, u32[]{:S(2)}) async-start(bf16[4,192,768]{2,1,0:T(8,128)(2,1)} %bitcast.172), calls=%async_computation.6 | async-start | bytes 2359296 | tf_op jit(solution)/shard_map/all_to_all | solution.py:40
  215.2 22.9 %copy-start.16 = (s32[12,2]{0,1:T(2,128)S(1)}, s32[12,2]{0,1:T(2,128)}, u32[]{:S(2)}) copy-start(s32[12,2]{0,1:T(2,128)} %param.26) | copy-start | bytes 292
  215.2 128.7 %all-to-all-start.8 = ((bf16[64,12,2304]{2,1,0:T(8,128)(2,1)}), bf16[64,12,2304]{2,1,0:T(8,128)(2,1)}, u32[]{:S(2)}, u32[]{:S(2)}) async-start(bf16[64,12,2304]{2,1,0:T(8,128)(2,1)} %stack.5), calls=%async_computation.8 | async-start | bytes 9437184 | tf_op jit(solution)/shard_map/all_to_all | solution.py:24
  345.1 3.7 copy-start.9
  345.1 3.9 copy-start.8
  345.1 4.0 copy-start.12
  345.1 4.0 copy-start.14
  345.1 5.0 %copy-start.20 = (s32[25]{0:T(128)S(1)}, s32[25]{0:T(128)}, u32[]{:S(2)}) copy-start(s32[25]{0:T(128)} %param.29) | copy-start | bytes 304
  345.1 18.0 %all-to-all-start.7 = ((bf16[4,192,768]{2,1,0:T(8,128)(2,1)}), bf16[4,192,768]{2,1,0:T(8,128)(2,1)S(1)}, u32[]{:S(2)}, u32[]{:S(2)}) async-start(bf16[4,192,768]{2,1,0:T(8,128)(2,1)} %broadcast_in_dim.112), calls=%async_computation.7 | async-start | bytes 2359296 | tf_op jit(solution)/shard_map/all_to_all | solution.py:30
  357.6 1.2 slice-start
  367.3 1.4 copy-start.2
  372.8 23.5 %copy-start.13 = (f32[768]{0:T(1024)S(1)}, f32[768]{0:T(1024)}, u32[]{:S(2)}) copy-start(f32[768]{0:T(1024)} %get-tuple-element.60) | copy-start | bytes 9220
  375.0 8.2 %all-to-all-start.9 = ((bf16[4,24,768]{2,1,0:T(8,128)(2,1)}), bf16[4,24,768]{2,1,0:T(8,128)(2,1)S(1)}, u32[]{:S(2)}, u32[]{:S(2)}) async-start(bf16[4,24,768]{2,1,0:T(8,128)(2,1)} %broadcast_in_dim.115), calls=%async_computation.9 | async-start | bytes 294912 | tf_op jit(solution)/shard_map/all_to_all | solution.py:30
  383.2 19.9 %all-to-all-start = ((bf16[64,2,128]{2,1,0:T(2,128)(2,1)}), bf16[64,2,128]{2,1,0:T(2,128)(2,1)S(1)}, u32[]{:S(2)}, u32[]{:S(2)}) async-start(bf16[64,2,128]{2,1,0:T(2,128)(2,1)} %copy.209), calls=%async_computation | async-start | bytes 65536 | tf_op jit(solution)/shard_map/all_to_all | solution.py:154
  396.4 10.8 %copy-start.7 = (bf16[1,56,256]{2,1,0:T(8,128)(2,1)S(1)}, bf16[1,56,256]{2,1,0:T(8,128)(2,1)}, u32[]{:S(2)}) copy-start(bf16[1,56,256]{2,1,0:T(8,128)(2,1)} %param.31) | copy-start | bytes 86020
  403.8 8.2 %all-to-all-start.10 = ((bf16[4,24,768]{2,1,0:T(8,128)(2,1)}), bf16[4,24,768]{2,1,0:T(8,128)(2,1)S(1)}, u32[]{:S(2)}, u32[]{:S(2)}) async-start(bf16[4,24,768]{2,1,0:T(8,128)(2,1)} %broadcast_in_dim.116), calls=%async_computation.10 | async-start | bytes 294912 | tf_op jit(solution)/shard_map/all_to_all | solution.py:30
  407.3 6.5 %copy-start.15 = (s32[12,1]{0,1:T(1,128)S(1)}, s32[12,1]{0,1:T(1,128)}, u32[]{:S(2)}) copy-start(s32[12,1]{0,1:T(1,128)} %param.25) | copy-start | bytes 148
  413.7 10.0 %copy-start.10 = (bf16[1,20,256]{2,1,0:T(8,128)(2,1)S(1)}, bf16[1,20,256]{2,1,0:T(8,128)(2,1)}, u32[]{:S(2)}) copy-start(bf16[1,20,256]{2,1,0:T(8,128)(2,1)} %param.32) | copy-start | bytes 30724
  416.1 19.0 %all-to-all-start.11 = ((bf16[64,2,768]{2,1,0:T(2,128)(2,1)}), bf16[64,2,768]{2,1,0:T(2,128)(2,1)S(1)}, u32[]{:S(2)}, u32[]{:S(2)}) async-start(bf16[64,2,768]{2,1,0:T(2,128)(2,1)} %reshape.384), calls=%async_computation.11 | async-start | bytes 393216 | tf_op jit(solution)/shard_map/all_to_all | solution.py:193
  423.9 12.8 %copy-start.18 = (bf16[1,256,256]{2,1,0:T(8,128)(2,1)S(1)}, bf16[1,256,256]{2,1,0:T(8,128)(2,1)}, u32[]{:S(2)}) copy-start(bf16[1,256,256]{2,1,0:T(8,128)(2,1)} %param.33) | copy-start | bytes 393220
  435.3 1.7 copy-start.17
  436.8 0.8 copy-start.19
  442.5 16.6 %all-to-all-start.12 = ((bf16[64,2,768]{2,1,0:T(2,128)(2,1)}), bf16[64,2,768]{2,1,0:T(2,128)(2,1)S(1)}, u32[]{:S(2)}, u32[]{:S(2)}) async-start(bf16[64,2,768]{2,1,0:T(2,128)(2,1)} %reshape.386), calls=%async_computation.12 | async-start | bytes 393216 | tf_op jit(solution)/shard_map/all_to_all | solution.py:215
